TPU v7x, 256 devices: a whole 4x4x8 slice. The times are simulated.
256 devices in a mesh: grp: 8 (over z), sub: 32 (over x, y, core).
Axes of the slice: x: 4, y: 4, z: 8, core: 2. Of those that a mesh axis runs over, the one named last changes fastest.
Arguments:
- residual: float32 [16, 98304], P(None, 'sub'), may hold values from -6 to 6
- margin: int32 [32, 8], replicated, may hold values from 0 to 767, as said below
- aggregate: int32 [768], P('sub'), may hold values from 0 to 63
- local_factor: bfloat16 [32, 4096, 4096], P('sub', 'grp'), may hold values from -0.09375 to 0.09375
- coarse_factor: bfloat16 [8192, 8192], P('sub'), may hold values from -0.0625 to 0.0625
Outputs:
- preconditioned: float32 [16, 98304], P('grp', 'sub')
Inputs may be any that keep to these rules, and one draw needn't show every extreme that they name: `margin`: for subdomain s, every entry names a block owned by another subdomain (block b is owned by subdomain b // 24); the entries of one row are distinct. Up to 8 entries of one row may name blocks of the same owner, and in every draw some row takes all of its entries from a single owner. `aggregate`: the counts of global blocks for each coarse block are whole numbers and may cross devices as int32.
All inputs are finite; a program needn't handle non-finite values.
Results may differ from a plain program's by a relative error of at most 0.0033.
Values sent between devices are 32-bit elements; how exact they have to be, the bound alone decides.
A program may use at most 64 MiB of HBM per device.

v0:
```python
import jax
import jax.numpy as jnp
from jax import lax
from jax.sharding import PartitionSpec as P

BLK = 128
NCB = 64


def row_of(table, index):
    return lax.dynamic_index_in_dim(table, index, 0, keepdims=False)


def on_device(residual, margin, aggregate, local_factor, coarse_factor):
    sub_count = lax.axis_size("sub")
    grp_count = lax.axis_size("grp")
    my_index = lax.axis_index("sub")
    grp_index = lax.axis_index("grp")
    rhs_count, own_width = residual.shape
    owned = own_width // BLK
    group_rows = rhs_count // grp_count
    blocks = residual.reshape(rhs_count, owned, BLK)
    exact = lax.Precision.HIGHEST
    my_list = row_of(margin, my_index)
    all_blocks = jnp.arange(owned * sub_count, dtype=jnp.int32)
    selector = (my_list[:, None] == all_blocks[None, :]).astype(jnp.float32)
    whole = lax.all_gather(blocks, "sub", axis=1, tiled=True)
    halo_rows = jnp.einsum("kb,rbc->rkc", selector, whole, precision=exact)
    local_rhs = (
        jnp.concatenate([blocks, halo_rows], axis=1).reshape(rhs_count, -1).astype(jnp.bfloat16)
    )
    factor = local_factor[0]
    inner_term = jnp.dot(local_rhs, factor.T, preferred_element_type=jnp.float32).astype(
        jnp.bfloat16
    )
    local_sol = lax.psum_scatter(
        jnp.dot(inner_term, factor, preferred_element_type=jnp.float32),
        "grp",
        scatter_dimension=0,
        tiled=True,
    )
    local_sol = local_sol.reshape(group_rows, -1, BLK)
    own_part = local_sol[:, :owned]
    back_rows = local_sol[:, owned:]
    spread = jnp.einsum("kb,rkc->rbc", selector, back_rows, precision=exact)
    returned = lax.psum_scatter(spread, "sub", scatter_dimension=1, tiled=True)
    catalog = jnp.arange(NCB, dtype=jnp.int32)
    member = (aggregate[:, None] == catalog[None, :]).astype(jnp.float32)
    mine = lax.dynamic_slice_in_dim(blocks, grp_index * group_rows, group_rows, 0)
    sums_part = jnp.einsum("rbk,bj->rjk", mine, member, precision=exact)
    sums, counts = lax.psum((sums_part, jnp.sum(member, axis=0)), "sub")
    coarse_rhs = (
        (sums / jnp.maximum(counts, 1.0)[None, :, None])
        .reshape(group_rows, -1)
        .astype(jnp.bfloat16)
    )
    inner_coarse = jnp.dot(coarse_rhs, coarse_factor.T, preferred_element_type=jnp.float32).astype(
        jnp.bfloat16
    )
    coarse_part = jnp.dot(inner_coarse, coarse_factor, preferred_element_type=jnp.float32)
    coarse_sol = lax.psum(coarse_part, "sub")
    prolonged = jnp.einsum(
        "rjk,bj->rbk", coarse_sol.reshape(group_rows, NCB, BLK), member, precision=exact
    )
    result = own_part + returned + prolonged
    return result.reshape(group_rows, -1)


def solution(mesh):
    placed = (P(None, "sub"), P(), P("sub"), P("sub", "grp", None), P("sub", None))
    return jax.shard_map(
        on_device, mesh=mesh, in_specs=placed, out_specs=P("grp", "sub"), check_vma=False
    )
```

profile of v0, /device:TPU:2, one launch (start us, length us, event | category | flops | bytes accessed | tf_op | source)
XLA Modules:
  0.0 460.0 jit_solution(2734043562929597561)
XLA Ops:
  6.5 1.0 copy.9
  7.5 1.6 convolution_bitcast_fusion.2
  9.2 0.7 all-gather.2.cloned.1.call-update
  10.0 0.2 dynamic-slice_reduce_fusion
  10.2 1.3 dynamic-slice
  12.1 0.7 convert_reduce_fusion
  12.8 55.4 %psum.22 = f32[64]{0:T(128)S(1)} all-reduce(f32[64]{0:T(128)S(1)} %convert_reduce_fusion), channel_id=1, replica_groups=mesh['grp'=8,'sub'=32] {'sub'}, use_global_device_ids=true, to_apply=%region_4.5 | all-reduce | flops 64 | bytes 512 | tf_op jit(solution)/shard_map/psum | solution.py:51
  68.3 0.9 bitcast_convert_fusion
  69.2 50.8 %all-reduce.5.cloned.1.call-done = f32[2,64,128]{2,1,0:T(8,128)} async-done(((f32[2,64,128]{2,1,0:T(8,128)}), f32[2,64,128]{2,1,0:T(8,128)}) %all-reduce.5.cloned.1.call-update) | async-done | bytes 65552 | tf_op jit(solution)/shard_map/psum | solution.py:51
  120.0 0.9 fusion.20
  120.9 54.7 %all-gather.2.cloned.1.call-done = f32[16,768,128]{2,1,0:T(8,128)} async-done(((f32[16,24,128]{2,1,0:T(8,128)}), f32[16,768,128]{2,1,0:T(8,128)}) %all-gather.2.cloned.1.call-update) | async-done | bytes 6291472 | tf_op jit(solution)/shard_map/all_gather | solution.py:27
  175.7 4.8 %fusion.4 = bf16[16,8,128]{2,1,0:T(8,128)(2,1)S(1)} fusion(f32[16,768,128]{2,1,0:T(8,128)} %all-gather.2.cloned.1.call-done, s32[8]{0:T(128)S(1)} %dynamic-slice_reduce_fusion), kind=kOutput, calls=%fused_computation.8 | convolution fusion | flops 151017472 | bytes 6324256 | tf_op jit(solution)/shard_map/kb,rbc->rkc/dot_general | solution.py:28
  180.5 6.0 %fusion = f32[16,4096]{1,0:T(8,128)} fusion(bf16[1,512,4096]{2,1,0:T(8,128)(2,1)} %param.8, bf16[2,8,32,128]{3,2,1,0:T(8,128)(2,1)S(1)} %bitcast.65), kind=kOutput, calls=%fused_computation | convolution fusion | flops 134225920 | bytes 4587520 | tf_op jit(solution)/shard_map/dot_general | solution.py:37
  186.6 0.0 all-reduce.7.cloned.1.call-start
  186.6 6.4 %convolution_bitcast_fusion.1 = f32[1,2,64,128]{3,1,2,0:T(2,128)S(1)} fusion(bf16[256,8192]{1,0:T(8,128)(2,1)} %param.9, bf16[1,2,64,128]{3,2,1,0:T(8,128)(2,1)S(1)} %fusion.20), kind=kOutput, calls=%fused_computation.5 | convolution fusion | flops 16777728 | bytes 4292608 | tf_op jit(solution)/shard_map/dot_general | solution.py:60
  193.0 0.6 copy.28
  193.6 0.0 reduce-scatter.2.cloned.1.call-start
  193.7 65.8 %all-reduce.9.cloned.1.call-done = f32[16,4096]{1,0:T(8,128)} async-done(((f32[16,4096]{1,0:T(8,128)}), f32[16,4096]{1,0:T(8,128)}) %all-reduce.9.cloned.1.call-update) | async-done | bytes 262160
  259.4 0.9 dynamic-slice_bitcast_fusion
  260.4 1.5 convolution_bitcast_fusion
  261.9 105.6 %all-reduce.7.cloned.1.call-done = f32[2,64,128]{2,1,0:T(8,128)} async-done(((f32[2,64,128]{2,1,0:T(8,128)}), f32[2,64,128]{2,1,0:T(8,128)}) %all-reduce.7.cloned.1.call-update) | async-done | bytes 65552 | tf_op jit(solution)/shard_map/psum | solution.py:61
  367.4 84.3 %reduce-scatter.2.cloned.1.call-done = f32[2,24,128]{2,1,0:T(8,128)} async-done(((f32[2,768,128]{2,1,0:T(8,128)}), f32[2,24,128]{2,1,0:T(8,128)}) %reduce-scatter.2.cloned.1.call-update) | async-done | bytes 24592 | tf_op jit(solution)/shard_map/reduce_scatter | solution.py:46
  451.8 1.0 fusion.11
  452.8 0.6 copy.30
  (16 shorter events, 0.2 us)
Async XLA Ops:
  6.5 3.5 copy-start
  6.5 113.4 %all-reduce.5.cloned.1.call-start = ((), (), s32[]{:S(2)}) async-start(), calls=%async_computation.3 | async-start | bytes 131072 | tf_op jit(solution)/shard_map/psum | solution.py:51
  7.5 1.7 copy-start.1
  9.2 166.5 %all-gather.2.cloned.1.call-start = ((), (), s32[]{:S(2)}) async-start(), calls=%async_computation.1 | async-start | bytes 6488064 | tf_op jit(solution)/shard_map/all_gather | solution.py:27
  9.9 249.5 %all-reduce.9.cloned.1.call-start = ((), (), s32[]{:S(2)}) async-start(), calls=%async_computation.5 | async-start | bytes 524288
  186.5 265.2 %copy-start.2 = (s32[24]{0:T(128)S(1)}, s32[24]{0:T(128)}, u32[]{:S(2)}) copy-start(s32[24]{0:T(128)} %param.7) | copy-start | bytes 292
  186.6 180.9 %all-reduce.7.cloned.1.call-start = ((), (), s32[]{:S(2)}) async-start(), calls=%async_computation.4 | async-start | bytes 131072 | tf_op jit(solution)/shard_map/psum | solution.py:61
  193.6 258.1 %reduce-scatter.2.cloned.1.call-start = ((), (), s32[]{:S(2)}) async-start(), calls=%async_computation.2 | async-start | bytes 811008 | tf_op jit(solution)/shard_map/reduce_scatter | solution.py:46
Sparse Core Ops, SparseCore 0:
  10.6 109.3 all-reduce.4
  122.7 52.9 all-gather.1
  186.7 72.7 all-reduce.8
  262.5 104.8 all-reduce.6
  371.1 80.6 reduce-scatter.1
where the time goes:
time: 460 us
  waiting for transfers between devices  362 us (79%)
  blocking collectives  55.4 us (12%)
  matrix products  21.3 us (5%)
  between operations  13.9 us (3%)
  local copies, waits for them, and re-layouts  4.62 us (1%)
    psum x1, waiting for transfers between devices, on_device(): coarse_sol = lax.psum(coarse_part, 'sub')  106 us
    reduce_scatter x1, waiting for transfers between devices, on_device(): returned = lax.psum_scatter(spread, 'sub', scatter_dimension=1, tiled=True)  84.3 us
    unnamed x6, waiting for transfers between devices  66.5 us
    psum x1, blocking collectives, on_device(): sums, counts = lax.psum((sums_part, jnp.sum(member, axis=0)), 'sub')  55.4 us
    all_gather x1, waiting for transfers between devices, on_device(): whole = lax.all_gather(blocks, 'sub', axis=1, tiled=True)  54.7 us
    psum x1, waiting for transfers between devices, on_device(): sums, counts = lax.psum((sums_part, jnp.sum(member, axis=0)), 'sub')  50.8 us
  transfers between devices with their start and end apart: 5, of which 5 were waited for; matrix products, arithmetic and copies ran while one was open for 3% of the time, Pallas kernels for 0%

commit v1 on v0

--- a/solution.py
+++ b/solution.py
@@ -24,7 +24,9 @@
     my_list = row_of(margin, my_index)
     all_blocks = jnp.arange(owned * sub_count, dtype=jnp.int32)
     selector = (my_list[:, None] == all_blocks[None, :]).astype(jnp.float32)
-    whole = lax.all_gather(blocks, "sub", axis=1, tiled=True)
+    whole = jnp.concatenate(
+        lax.all_to_all(jnp.stack([blocks] * lax.axis_size("sub")), "sub", 0, 0), axis=1
+    )
     halo_rows = jnp.einsum("kb,rbc->rkc", selector, whole, precision=exact)
     local_rhs = (
         jnp.concatenate([blocks, halo_rows], axis=1).reshape(rhs_count, -1).astype(jnp.bfloat16)

time: 460 us -> 374 us (0.81)
  waiting for transfers between devices: 362 us -> 193 us
  blocking collectives: 55.4 us -> 125 us
  starting transfers between devices: 0.17 us -> 7.98 us
  local copies, waits for them, and re-layouts: 4.62 us -> 10.7 us
    reduce_scatter x1, waiting for transfers between devices: 84.3 us -> 0.01 us  [on_device(): returned = lax.psum_scatter(spread, 'sub', scatter_dimension=1, tiled=True)]
    psum x1, blocking collectives: 55.4 us -> 125 us  [on_device(): sums, counts = lax.psum((sums_part, jnp.sum(member, axis=0)), 'sub')]
    all_gather x1 -> x0, waiting for transfers between devices: 54.7 us -> none  [on_device(): whole = lax.all_gather(blocks, 'sub', axis=1, tiled=True)]
    psum x1, waiting for transfers between devices: 50.8 us -> 22.3 us  [on_device(): sums, counts = lax.psum((sums_part, jnp.sum(member, axis=0)), 'sub')]
    all_to_all x0 -> x1, starting transfers between devices: none -> 7.81 us  [on_device(): lax.all_to_all(jnp.stack([blocks] * lax.axis_size('sub')), 'sub', 0, 0)]
    unnamed x6 -> x5, waiting for transfers between devices: 66.5 us -> 65.6 us
  transfers between devices with their start and end apart: 5 -> 5, of which waited for: 5 -> 3; matrix products, arithmetic and copies ran while one was open for 3% -> 3% of each run, Pallas kernels for 0% -> 0%
where the time goes in v1:
time: 374 us; the launch traced here: 371 us
  waiting for transfers between devices  193 us (52%)
  blocking collectives  125 us (33%)
  matrix products  17.9 us (5%)
  between operations  15.6 us (4%)
  local copies, waits for them, and re-layouts  10.7 us (3%)
  starting transfers between devices  7.98 us (2%)
    psum x1, blocking collectives, on_device(): sums, counts = lax.psum((sums_part, jnp.sum(member, axis=0)), 'sub')  125 us
    psum x1, waiting for transfers between devices, on_device(): coarse_sol = lax.psum(coarse_part, 'sub')  105 us
    unnamed x5, waiting for transfers between devices  65.6 us
    psum x1, waiting for transfers between devices, on_device(): sums, counts = lax.psum((sums_part, jnp.sum(member, axis=0)), 'sub')  22.3 us
    all_to_all x1, starting transfers between devices, on_device(): lax.all_to_all(jnp.stack([blocks] * lax.axis_size('sub')), 'sub', 0, 0)  7.81 us
  transfers between devices with their start and end apart: 5, of which 3 were waited for; matrix products, arithmetic and copies ran while one was open for 3% of the time, Pallas kernels for 0%

profile of v1, /device:TPU:2, one launch (start us, length us, event | category | flops | bytes accessed | tf_op | source)
XLA Modules:
  0.0 371.5 jit_solution(944263574681960436)
XLA Ops:
  7.4 1.0 copy.10
  8.4 3.4 stack.3
  11.7 7.8 %all-to-all-start = ((f32[32,16,24,128]{3,2,1,0:T(8,128)}), f32[32,16,24,128]{3,2,1,0:T(8,128)}, u32[]{:S(2)}, u32[]{:S(2)}) async-start(f32[32,16,24,128]{3,2,1,0:T(8,128)} %stack.3), calls=%async_computation | async-start | bytes 12582912 | tf_op jit(solution)/shard_map/all_to_all | solution.py:28
  19.6 0.9 convolution_bitcast_fusion.2
  20.5 0.0 all-reduce.9.cloned.1.call-start
  20.6 0.1 convert_reduce_fusion
  20.7 125.0 %psum.22 = f32[64]{0:T(128)S(1)} all-reduce(f32[64]{0:T(128)S(1)} %convert_reduce_fusion), channel_id=1, replica_groups=mesh['grp'=8,'sub'=32] {'sub'}, use_global_device_ids=true, to_apply=%region_4.5 | all-reduce | flops 64 | bytes 512 | tf_op jit(solution)/shard_map/psum | solution.py:53
  145.7 0.6 dynamic-slice
  146.9 0.2 dynamic-slice_reduce_fusion
  147.1 22.3 %all-reduce.5.cloned.1.call-done = f32[2,64,128]{2,1,0:T(8,128)} async-done(((f32[2,64,128]{2,1,0:T(8,128)}), f32[2,64,128]{2,1,0:T(8,128)}) %all-reduce.5.cloned.1.call-update) | async-done | bytes 65552 | tf_op jit(solution)/shard_map/psum | solution.py:53
  169.5 0.9 fusion.20
  170.4 3.4 copy.7
  173.8 2.2 fusion.4
  176.0 6.0 %fusion = f32[16,4096]{1,0:T(8,128)} fusion(bf16[1,512,4096]{2,1,0:T(8,128)(2,1)} %param.8, bf16[2,8,32,128]{3,2,1,0:T(8,128)(2,1)S(1)} %bitcast.68), kind=kOutput, calls=%fused_computation | convolution fusion | flops 134225920 | bytes 4587520 | tf_op jit(solution)/shard_map/dot_general | solution.py:39
  182.0 0.0 all-reduce.7.cloned.1.call-start
  182.1 6.4 %convolution_bitcast_fusion.1 = f32[1,2,64,128]{3,1,2,0:T(2,128)S(1)} fusion(bf16[256,8192]{1,0:T(8,128)(2,1)} %param.9, bf16[1,2,64,128]{3,2,1,0:T(8,128)(2,1)S(1)} %fusion.20), kind=kOutput, calls=%fused_computation.5 | convolution fusion | flops 16777728 | bytes 4292608 | tf_op jit(solution)/shard_map/dot_general | solution.py:62
  188.4 0.6 copy.29
  189.1 0.0 reduce-scatter.2.cloned.1.call-start
  189.1 65.6 %all-reduce.9.cloned.1.call-done = f32[16,4096]{1,0:T(8,128)} async-done(((f32[16,4096]{1,0:T(8,128)}), f32[16,4096]{1,0:T(8,128)}) %all-reduce.9.cloned.1.call-update) | async-done | bytes 262160
  254.7 0.9 dynamic-slice_bitcast_fusion
  255.6 1.5 convolution_bitcast_fusion
  257.1 105.2 %all-reduce.7.cloned.1.call-done = f32[2,64,128]{2,1,0:T(8,128)} async-done(((f32[2,64,128]{2,1,0:T(8,128)}), f32[2,64,128]{2,1,0:T(8,128)}) %all-reduce.7.cloned.1.call-update) | async-done | bytes 65552 | tf_op jit(solution)/shard_map/psum | solution.py:63
  362.4 1.0 fusion.11
  363.4 0.6 copy.31
  (17 shorter events, 0.2 us)
Async XLA Ops:
  7.4 139.6 %copy-start = (s32[32,8]{0,1:T(8,128)S(1)}, s32[32,8]{0,1:T(8,128)}, u32[]{:S(2)}) copy-start(s32[32,8]{0,1:T(8,128)} %param.6) | copy-start | bytes 3076
  11.7 7.9 %copy-start.1 = (s32[24]{0:T(128)S(1)}, s32[24]{0:T(128)}, u32[]{:S(2)}) copy-start(s32[24]{0:T(128)} %param.7) | copy-start | bytes 292
  11.7 134.0 %copy-start.2 = (u32[256]{0:T(256)S(1)}, u32[256]{0:T(256)}, u32[]{:S(2)}) copy-start(u32[256]{0:T(256)} %constant.28) | copy-start | bytes 3076
  11.7 158.7 %all-to-all-start = ((f32[32,16,24,128]{3,2,1,0:T(8,128)}), f32[32,16,24,128]{3,2,1,0:T(8,128)}, u32[]{:S(2)}, u32[]{:S(2)}) async-start(f32[32,16,24,128]{3,2,1,0:T(8,128)} %stack.3), calls=%async_computation | async-start | bytes 12582912 | tf_op jit(solution)/shard_map/all_to_all | solution.py:28
  19.5 149.9 %all-reduce.5.cloned.1.call-start = ((), (), s32[]{:S(2)}) async-start(), calls=%async_computation.3 | async-start | bytes 131072 | tf_op jit(solution)/shard_map/psum | solution.py:53
  20.5 234.2 %all-reduce.9.cloned.1.call-start = ((), (), s32[]{:S(2)}) async-start(), calls=%async_computation.5 | async-start | bytes 524288
  182.0 180.3 %all-reduce.7.cloned.1.call-start = ((), (), s32[]{:S(2)}) async-start(), calls=%async_computation.4 | async-start | bytes 131072 | tf_op jit(solution)/shard_map/psum | solution.py:63
  189.1 173.3 %reduce-scatter.2.cloned.1.call-start = ((), (), s32[]{:S(2)}) async-start(), calls=%async_computation.2 | async-start | bytes 811008 | tf_op jit(solution)/shard_map/reduce_scatter | solution.py:48
Sparse Core Ops, SparseCore 0:
  23.6 145.8 all-reduce.4
  257.3 79.3 reduce-scatter.1
Sparse Core Ops, SparseCore 1:
  182.1 72.5 all-reduce.8
  257.8 104.5 all-reduce.6
